TPU v7x, 32 devices: a whole 2x2x4 slice. The times are simulated.
32 devices in a mesh: dp: 8 (over y, x, core), fsdp: 4 (over z).
Axes of the slice: x: 2, y: 2, z: 4, core: 2. Of those that a mesh axis runs over, the one named last changes fastest.
Arguments:
- tokens: bfloat16 [16384, 1024], P(('dp', 'fsdp')), may hold values from -20 to 20
- w_qkv: bfloat16 [1024, 3072], P('fsdp'), may hold values from -0.1875 to 0.1875
- w_out: bfloat16 [1024, 1024], P('fsdp'), may hold values from -0.1875 to 0.1875
- doc_blocks: int32 [32, 4], P(('dp', 'fsdp')), may hold values from 0 to 1, never falling along the last dimension, each value on 1 to 3 neighbouring positions
- cotangent: bfloat16 [16384, 1024], P(('dp', 'fsdp')), may hold values from -6 to 6
Outputs:
- output: bfloat16 [16384, 1024], P(('dp', 'fsdp'))
- grad_tokens: bfloat16 [16384, 1024], P(('dp', 'fsdp'))
- grad_w_qkv: float32 [1024, 3072], P('fsdp')
- grad_w_out: float32 [1024, 1024], P('fsdp')
Inputs may be any that keep to these rules, and one draw needn't show every extreme that they name: `doc_blocks`: ids never fall along a sequence; each of the 2 documents of a sequence covers 1 to 3 blocks.
All inputs are finite; a program needn't handle non-finite values.
Results may differ from a plain program's by a relative error of at most 0.012.
Values may be sent and summed in bfloat16 or wider, within the bound.
A program may use at most 128 MiB of HBM per device.

v0:
```python
import math
import jax
import jax.numpy as jnp
from jax import lax
from jax.sharding import PartitionSpec as P

H = 8
NEG_FILL = -1e30
CONTRACT_ROWS = (((0,), (0,)), ((), ()))
CONTRACT_COLS = (((1,), (1,)), ((), ()))


def row_mask(doc_ids, row_count):
    block_len = row_count // doc_ids.shape[0]
    doc_rows = jnp.repeat(doc_ids, block_len, total_repeat_length=row_count)
    position = jnp.arange(row_count, dtype=jnp.int32)
    causal = position[None, :] <= position[:, None]
    return causal & (doc_rows[None, :] == doc_rows[:, None])


def split_heads(matrix, head_count):
    return matrix.reshape(matrix.shape[0], head_count, matrix.shape[1] // head_count)


def attend_forward(query_rows, key_rows, value_rows, allowed, head_count):
    row_count = query_rows.shape[0]
    query_heads = split_heads(query_rows, head_count)
    key_heads = split_heads(key_rows, head_count)
    value_heads = split_heads(value_rows, head_count)
    score_scale = query_heads.shape[2] ** (-0.5)
    scores = (
        jnp.einsum("qhd,khd->hqk", query_heads, key_heads, preferred_element_type=jnp.float32)
        * score_scale
    )
    scores = jnp.where(allowed[None], scores, NEG_FILL)
    highest = jnp.max(scores, axis=-1, keepdims=True)
    expvals = jnp.exp(scores - highest)
    attn_probs = expvals / jnp.sum(expvals, axis=-1, keepdims=True)
    probs_half = attn_probs.astype(jnp.bfloat16)
    mixed = jnp.einsum("hqk,khd->qhd", probs_half, value_heads, preferred_element_type=jnp.float32)
    return (mixed.astype(jnp.bfloat16).reshape(row_count, -1), attn_probs, probs_half)


def attend_backward(
    query_rows, key_rows, value_rows, attn_probs, probs_half, grad_mixed, head_count
):
    row_count = query_rows.shape[0]
    query_heads = split_heads(query_rows, head_count)
    key_heads = split_heads(key_rows, head_count)
    value_heads = split_heads(value_rows, head_count)
    grad_heads = split_heads(grad_mixed, head_count)
    score_scale = query_heads.shape[2] ** (-0.5)
    grad_probs = jnp.einsum(
        "qhd,khd->hqk", grad_heads, value_heads, preferred_element_type=jnp.float32
    )
    grad_values = jnp.einsum(
        "hqk,qhd->khd", probs_half, grad_heads, preferred_element_type=jnp.float32
    )
    inner = jnp.sum(attn_probs * grad_probs, axis=-1, keepdims=True)
    grad_scores = (attn_probs * (grad_probs - inner)).astype(jnp.bfloat16)
    grad_queries = (
        jnp.einsum("hqk,khd->qhd", grad_scores, key_heads, preferred_element_type=jnp.float32)
        * score_scale
    )
    grad_keys = (
        jnp.einsum("hqk,qhd->khd", grad_scores, query_heads, preferred_element_type=jnp.float32)
        * score_scale
    )
    pieces_list = [grad_queries, grad_keys, grad_values]
    return jnp.concatenate(
        [p.astype(jnp.bfloat16).reshape(row_count, -1) for p in pieces_list], axis=1
    )


def body(tokens, w_qkv, w_out, doc_blocks, cotangent):
    row_count = tokens.shape[0]
    head_width = w_out.shape[1]
    head_count = H
    all_devices = lax.axis_size("dp") * lax.axis_size("fsdp")
    allowed = row_mask(doc_blocks[0], row_count)
    columns = tokens
    qkv = jnp.dot(
        columns,
        lax.all_gather(w_qkv, "fsdp", axis=0, tiled=True),
        preferred_element_type=jnp.float32,
    ).astype(jnp.bfloat16)
    query_rows = qkv[:, :head_width]
    key_rows = qkv[:, head_width : 2 * head_width]
    value_rows = qkv[:, 2 * head_width :]
    mixed, attn_probs, probs_half = attend_forward(
        query_rows, key_rows, value_rows, allowed, head_count
    )
    output = lax.dot_general(
        mixed,
        lax.all_gather(w_out, "fsdp", axis=0, tiled=True),
        CONTRACT_COLS,
        preferred_element_type=jnp.float32,
    )
    columns = cotangent
    grad_mixed = jnp.dot(
        columns,
        lax.all_gather(w_out, "fsdp", axis=0, tiled=True),
        preferred_element_type=jnp.float32,
    ).astype(jnp.bfloat16)
    output = output.astype(jnp.bfloat16)
    grad_qkv = attend_backward(
        query_rows, key_rows, value_rows, attn_probs, probs_half, grad_mixed, head_count
    )
    grad_tokens = lax.dot_general(
        grad_qkv,
        lax.all_gather(w_qkv, "fsdp", axis=0, tiled=True),
        CONTRACT_COLS,
        preferred_element_type=jnp.float32,
    )
    grad_tokens = grad_tokens.astype(jnp.bfloat16)
    first_term = lax.dot_general(
        tokens, grad_qkv, CONTRACT_ROWS, preferred_element_type=jnp.float32
    )
    second_term = lax.dot_general(
        cotangent, mixed, CONTRACT_ROWS, preferred_element_type=jnp.float32
    )
    partial_grad = lax.psum_scatter(
        jnp.concatenate([first_term, second_term], axis=1), "fsdp", scatter_dimension=0, tiled=True
    )
    summed = lax.psum(partial_grad, "dp")
    norm_factor = 1.0 / math.sqrt(row_count * all_devices)
    grad_w_qkv = summed[:, : 3 * head_width] * norm_factor
    grad_w_out = summed[:, 3 * head_width :] * norm_factor
    return (output, grad_tokens, grad_w_qkv, grad_w_out)


def solution(mesh):
    placed = (
        P(("dp", "fsdp"), None),
        P("fsdp", None),
        P("fsdp", None),
        P(("dp", "fsdp"), None),
        P(("dp", "fsdp"), None),
    )
    return jax.shard_map(
        body,
        mesh=mesh,
        in_specs=placed,
        out_specs=(
            P(("dp", "fsdp"), None),
            P(("dp", "fsdp"), None),
            P("fsdp", None),
            P("fsdp", None),
        ),
        check_vma=False,
    )
```

profile of v0, /device:TPU:0, one launch (start us, length us, event | category | flops | bytes accessed | tf_op | source)
XLA Modules:
  0.0 596.9 jit_solution(12965069515736910643)
XLA Ops:
  7.2 0.0 copy-start
  7.2 0.0 all-gather.5.cloned.1.call-start
  7.2 0.7 all-gather.5.cloned.1.call-update
  7.9 0.0 all-gather.3.cloned.1.call-start
  8.0 0.7 all-gather.3.cloned.1.call-update
  8.7 0.0 reduce-scatter.2.cloned.1.call-start
  8.7 1.4 fusion.30
  10.1 2.6 compare_select_fusion.1
  12.7 0.2 fusion.18
  13.0 45.0 %all-gather.5.cloned.1.call-done = bf16[1024,1024]{1,0:T(8,128)(2,1)} async-done(((bf16[256,1024]{1,0:T(8,128)(2,1)}), bf16[1024,1024]{1,0:T(8,128)(2,1)}) %all-gather.5.cloned.1.call-update) | async-done | bytes 2097168 | tf_op jit(solution)/shard_map/all_gather | solution.py:95
  58.0 3.2 convolution_convert_fusion.1
  61.1 1.3 copy.29
  62.5 111.2 %all-gather.3.cloned.1.call-done = bf16[1024,3072]{1,0:T(8,128)(2,1)} async-done(((bf16[256,3072]{1,0:T(8,128)(2,1)}), bf16[1024,3072]{1,0:T(8,128)(2,1)}) %all-gather.3.cloned.1.call-update) | async-done | bytes 6291472 | tf_op jit(solution)/shard_map/all_gather | solution.py:84
  173.7 0.0 copy-done
  173.7 6.4 %convolution_convert_fusion = bf16[512,3072]{1,0:T(8,128)(2,1)S(1)} fusion(bf16[512,1024]{1,0:T(8,128)(2,1)S(1)} %copy-done, bf16[1024,3072]{1,0:T(8,128)(2,1)} %all-gather.3.cloned.1.call-done), kind=kOutput, calls=%fused_computation.8 | convolution fusion | flops 3222798336 | bytes 10485760 | tf_op jit(solution)/shard_map/dot_general | solution.py:82
  180.1 1.8 fusion.29
  181.9 0.5 copy.27
  182.5 1.5 copy.28
  184.0 5.4 fusion.31
  189.4 0.0 copy-start.1
  189.4 0.0 copy-start.2
  189.4 4.7 fusion.9
  194.1 0.0 copy-start.9
  194.2 1.7 copy-done.1
  195.9 0.2 copy-done.2
  196.1 0.0 copy-start.5
  196.1 1.5 fusion.12
  197.6 0.0 copy-done.5
  197.6 0.0 copy-start.7
  197.7 1.5 multiply_reduce_fusion
  199.2 2.7 multiply_convert_fusion
  201.9 1.5 multiply_convert_fusion.1
  203.4 0.0 copy-start.3
  203.4 0.0 copy-start.6
  203.4 0.7 multiply_convert_fusion.2
  204.1 0.0 copy-done.9
  204.1 0.9 copy-done.6
  205.0 1.3 convolution_bitcast_fusion.1
  206.3 0.0 copy-done.7
  206.3 0.0 copy-done.3
  206.3 3.5 convolution_bitcast_fusion
  209.8 7.2 %pad_maximum_fusion = f32[1024,4096]{0,1:T(8,128)} fusion(f32[1024,1024]{0,1:T(8,128)S(1)} %convolution_bitcast_fusion.1, f32[1024,3072]{0,1:T(8,128)S(1)} %convolution_bitcast_fusion), kind=kLoop, calls=%fused_computation.1 | loop fusion | flops 4194304 | bytes 33554432 | tf_op jit(solution)/shard_map/concatenate | solution.py:123
  217.1 0.0 reduce-scatter.2.cloned.1.call-update
  217.1 0.0 copy-start.10
  217.1 0.0 all-reduce.2.cloned.1.call-start
  217.2 278.7 %reduce-scatter.2.cloned.1.call-done = f32[256,4096]{0,1:T(8,128)} async-done(((f32[1024,4096]{0,1:T(8,128)}), f32[256,4096]{0,1:T(8,128)}) %reduce-scatter.2.cloned.1.call-update) | async-done | bytes 4194320 | tf_op jit(solution)/shard_map/reduce_scatter | solution.py:122
  495.8 0.0 all-reduce.2.cloned.1.call-update
  495.9 0.0 copy-done.10
  495.9 0.0 copy-start.4
  495.9 0.0 copy-start.8
  495.9 4.0 convolution_convert_fusion.2
  499.9 0.0 copy-done.4
  499.9 0.0 copy-done.8
  499.9 7.2 %convolution_convert_fusion.3 = bf16[512,1024]{1,0:T(8,128)(2,1)} fusion(bf16[1024,3072]{1,0:T(8,128)(2,1)} %all-gather.3.cloned.1.call-done, bf16[512,1024]{0,1:T(8,128)(2,1)S(1)} %bitcast.77, bf16[512,1024]{0,1:T(8,128)(2,1)S(1)} %bitcast.70, bf16[512,1024]{0,1:T(8,128)(2,1)S(1)} %bitcast.72), kind=kOutput, calls=%fused_computation.26 | convolution fusion | flops 3231186944 | bytes 10485760 | tf_op jit(solution)/shard_map/dot_general | solution.py:109
  507.1 73.3 %all-reduce.2.cloned.1.call-done = f32[256,4096]{0,1:T(8,128)} async-done(((f32[256,4096]{0,1:T(8,128)}), f32[256,4096]{0,1:T(8,128)}) %all-reduce.2.cloned.1.call-update) | async-done | bytes 4194320 | tf_op jit(solution)/shard_map/psum | solution.py:125
  580.4 3.8 slice_multiply_fusion
  584.2 3.5 copy.21
  587.8 1.3 slice_multiply_fusion.1
  589.1 1.3 copy.22
  (3 shorter events, 0.0 us)
Async XLA Ops:
  7.2 166.5 %copy-start = (bf16[512,1024]{1,0:T(8,128)(2,1)S(1)}, bf16[512,1024]{1,0:T(8,128)(2,1)}, u32[]{:S(2)}) copy-start(bf16[512,1024]{1,0:T(8,128)(2,1)} %param.7) | copy-start | bytes 3145732
  7.2 50.8 %all-gather.5.cloned.1.call-start = ((), (), s32[]{:S(2)}) async-start(), calls=%async_computation.2 | async-start | bytes 2621440 | tf_op jit(solution)/shard_map/all_gather | solution.py:95
  7.9 165.8 %all-gather.3.cloned.1.call-start = ((), (), s32[]{:S(2)}) async-start(), calls=%async_computation.1 | async-start | bytes 7864320 | tf_op jit(solution)/shard_map/all_gather | solution.py:84
  8.7 487.2 %reduce-scatter.2.cloned.1.call-start = ((), (), s32[]{:S(2)}) async-start(), calls=%async_computation.3 | async-start | bytes 20971520 | tf_op jit(solution)/shard_map/reduce_scatter | solution.py:122
  189.4 6.5 %copy-start.1 = (f32[8,512,512]{1,2,0:T(8,128)S(1)}, f32[8,512,512]{1,2,0:T(8,128)}, u32[]{:S(2)}) copy-start(f32[8,512,512]{1,2,0:T(8,128)} %get-tuple-element.28) | copy-start | bytes 25165828
  189.4 6.7 %copy-start.2 = (bf16[512,1024]{0,1:T(8,128)(2,1)S(1)}, bf16[512,1024]{0,1:T(8,128)(2,1)}, u32[]{:S(2)}) copy-start(bf16[512,1024]{0,1:T(8,128)(2,1)} %copy.29) | copy-start | bytes 3145732
  194.1 10.0 %copy-start.9 = (bf16[8,128,512]{2,1,0:T(8,128)(2,1)}, bf16[8,128,512]{2,1,0:T(8,128)(2,1)S(1)}, u32[]{:S(2)}) copy-start(bf16[8,128,512]{2,1,0:T(8,128)(2,1)S(1)} %fusion.9) | copy-start | bytes 3145732
  196.1 1.5 copy-start.5
  197.6 8.6 %copy-start.7 = (bf16[8,128,512]{2,1,0:T(8,128)(2,1)}, bf16[8,128,512]{2,1,0:T(8,128)(2,1)S(1)}, u32[]{:S(2)}) copy-start(bf16[8,128,512]{2,1,0:T(8,128)(2,1)S(1)} %fusion.12) | copy-start | bytes 3145732
  203.4 2.9 copy-start.3
  203.4 1.6 copy-start.6
  217.1 278.8 %copy-start.10 = (bf16[8,128,512]{2,1,0:T(8,128)(2,1)S(1)}, bf16[8,128,512]{2,1,0:T(8,128)(2,1)}, u32[]{:S(2)}) copy-start(bf16[8,128,512]{2,1,0:T(8,128)(2,1)} %copy-done.9) | copy-start | bytes 3145732
  217.1 363.3 %all-reduce.2.cloned.1.call-start = ((), (), s32[]{:S(2)}) async-start(), calls=%async_computation.4 | async-start | bytes 8388608 | tf_op jit(solution)/shard_map/psum | solution.py:125
  495.9 4.0 copy-start.4
  495.9 4.0 copy-start.8
Sparse Core Ops, SparseCore 0:
  9.6 48.3 all-gather.4
  59.5 114.1 all-gather.2
  217.2 278.5 reduce-scatter.1
  499.0 81.4 all-reduce.1
where the time goes:
time: 597 us
  waiting for transfers between devices  510 us (85%)
  matrix products  41 us (7%)
  other arithmetic  17.8 us (3%)
  local copies, waits for them, and re-layouts  14.3 us (2%)
  between operations  14 us (2%)
    reduce_scatter x1, waiting for transfers between devices, body(): lax.psum_scatter(jnp.concatenate([first_term, second_term], axis=1), 'fsd...  279 us
    all_gather x1, waiting for transfers between devices, body(): lax.all_gather(w_qkv, 'fsdp', axis=0, tiled=True)  111 us
    psum x1, waiting for transfers between devices, body(): summed = lax.psum(partial_grad, 'dp')  73.3 us
    all_gather x1, waiting for transfers between devices, body(): lax.all_gather(w_out, 'fsdp', axis=0, tiled=True)  45 us
  transfers between devices with their start and end apart: 4, of which 4 were waited for; matrix products, arithmetic and copies ran while one was open for 3% of the time, Pallas kernels for 0%

commit v1 on v0

--- a/solution.py
+++ b/solution.py
@@ -122,7 +122,9 @@
     partial_grad = lax.psum_scatter(
         jnp.concatenate([first_term, second_term], axis=1), "fsdp", scatter_dimension=0, tiled=True
     )
-    summed = lax.psum(partial_grad, "dp")
+    summed = partial_grad
+    for hop in (1, 2, 4):
+        summed = summed + lax.ppermute(summed, "dp", [(dev, dev ^ hop) for dev in range(8)])
     norm_factor = 1.0 / math.sqrt(row_count * all_devices)
     grad_w_qkv = summed[:, : 3 * head_width] * norm_factor
     grad_w_out = summed[:, 3 * head_width :] * norm_factor

time: 597 us -> 706 us (1.18)
  waiting for transfers between devices: 510 us -> 619 us
    ppermute x0 -> x3, waiting for transfers between devices: none -> 182 us  [body(): lax.ppermute(summed, 'dp', [(dev, dev ^ hop) for dev in range(8)])]
    psum x1 -> x0, waiting for transfers between devices: 73.3 us -> none  [body(): summed = lax.psum(partial_grad, 'dp')]
  transfers between devices with their start and end apart: 4 -> 6, of which waited for: 4 -> 6; matrix products, arithmetic and copies ran while one was open for 3% -> 2% of each run, Pallas kernels for 0% -> 0%
where the time goes in v1:
time: 706 us; the launch traced here: 705 us
  waiting for transfers between devices  619 us (88%)
  matrix products  36.6 us (5%)
  other arithmetic  18.6 us (3%)
  local copies, waits for them, and re-layouts  14.4 us (2%)
  between operations  14 us (2%)
    reduce_scatter x1, waiting for transfers between devices, body(): lax.psum_scatter(jnp.concatenate([first_term, second_term], axis=1), 'fsd...  279 us
    ppermute x3, waiting for transfers between devices, body(): lax.ppermute(summed, 'dp', [(dev, dev ^ hop) for dev in range(8)])  182 us
    all_gather x1, waiting for transfers between devices, body(): lax.all_gather(w_qkv, 'fsdp', axis=0, tiled=True)  111 us
    all_gather x1, waiting for transfers between devices, body(): lax.all_gather(w_out, 'fsdp', axis=0, tiled=True)  45 us
  transfers between devices with their start and end apart: 6, of which 6 were waited for; matrix products, arithmetic and copies ran while one was open for 2% of the time, Pallas kernels for 0%

profile of v1, /device:TPU:0, one launch (start us, length us, event | category | flops | bytes accessed | tf_op | source)
XLA Modules:
  0.0 705.2 jit_solution(4440395424994972814)
XLA Ops:
  7.2 0.0 copy-start
  7.2 0.0 all-gather.5.cloned.1.call-start
  7.2 0.7 all-gather.5.cloned.1.call-update
  7.9 0.0 all-gather.3.cloned.1.call-start
  8.0 0.7 all-gather.3.cloned.1.call-update
  8.7 0.0 reduce-scatter.2.cloned.1.call-start
  8.7 1.4 fusion.30
  10.1 2.6 compare_select_fusion.1
  12.7 0.2 fusion.18
  13.0 45.0 %all-gather.5.cloned.1.call-done = bf16[1024,1024]{1,0:T(8,128)(2,1)} async-done(((bf16[256,1024]{1,0:T(8,128)(2,1)}), bf16[1024,1024]{1,0:T(8,128)(2,1)}) %all-gather.5.cloned.1.call-update) | async-done | bytes 2097168 | tf_op jit(solution)/shard_map/all_gather | solution.py:95
  58.0 3.2 convolution_convert_fusion.1
  61.1 1.3 copy.29
  62.5 111.2 %all-gather.3.cloned.1.call-done = bf16[1024,3072]{1,0:T(8,128)(2,1)} async-done(((bf16[256,3072]{1,0:T(8,128)(2,1)}), bf16[1024,3072]{1,0:T(8,128)(2,1)}) %all-gather.3.cloned.1.call-update) | async-done | bytes 6291472 | tf_op jit(solution)/shard_map/all_gather | solution.py:84
  173.7 0.0 copy-done
  173.7 6.4 convolution_convert_fusion
  180.1 1.8 fusion.29
  181.9 0.5 copy.27
  182.5 1.5 copy.28
  184.0 5.4 fusion.31
  189.4 4.7 fusion.9
  194.2 0.0 copy-start.11
  194.2 1.7 copy-done.2
  195.9 0.2 copy-done.3
  196.1 1.5 fusion.12
  197.7 0.0 copy-done.6
  197.7 0.0 copy-start.9
  197.7 1.5 multiply_reduce_fusion
  199.2 2.7 multiply_convert_fusion
  201.9 1.5 multiply_convert_fusion.1
  203.4 0.0 copy-start.4
  203.4 0.0 copy-start.8
  203.5 0.7 multiply_convert_fusion.2
  204.2 0.0 copy-done.11
  204.2 0.9 copy-done.8
  205.0 1.3 convolution_bitcast_fusion.1
  206.3 0.0 copy-done.9
  206.3 0.0 copy-done.4
  206.3 3.5 convolution_bitcast_fusion
  209.9 7.2 %pad_maximum_fusion = f32[1024,4096]{0,1:T(8,128)} fusion(f32[1024,1024]{0,1:T(8,128)S(1)} %convolution_bitcast_fusion.1, f32[1024,3072]{0,1:T(8,128)S(1)} %convolution_bitcast_fusion), kind=kLoop, calls=%fused_computation.1 | loop fusion | flops 4194304 | bytes 33554432 | tf_op jit(solution)/shard_map/concatenate | solution.py:123
  217.0 0.0 reduce-scatter.2.cloned.1.call-update
  217.1 278.9 %reduce-scatter.2.cloned.1.call-done = f32[256,4096]{0,1:T(8,128)} async-done(((f32[1024,4096]{0,1:T(8,128)}), f32[256,4096]{0,1:T(8,128)}) %reduce-scatter.2.cloned.1.call-update) | async-done | bytes 4194320 | tf_op jit(solution)/shard_map/reduce_scatter | solution.py:122
  495.9 0.0 collective-permute-start
  495.9 7.4 %collective-permute-done = f32[256,4096]{0,1:T(8,128)S(1)} collective-permute-done((f32[256,4096]{0,1:T(8,128)}, f32[256,4096]{0,1:T(8,128)S(1)}, u32[]{:S(2)}, u32[]{:S(2)}) %collective-permute-start) | collective-permute-done | bytes 4194336 | tf_op jit(solution)/shard_map/ppermute | solution.py:127
  503.3 2.9 add.78
  506.2 0.0 copy-start.7
  506.2 0.0 copy-start.12
  506.2 0.0 slice-start.1
  506.2 1.5 collective-permute-start.1
  507.8 91.1 %collective-permute-done.1 = f32[256,4096]{0,1:T(8,128)S(1)} collective-permute-done((f32[256,4096]{0,1:T(8,128)S(1)}, f32[256,4096]{0,1:T(8,128)S(1)}, u32[]{:S(2)}, u32[]{:S(2)}) %collective-permute-start.1) | collective-permute-done | bytes 4194336 | tf_op jit(solution)/shard_map/ppermute | solution.py:127
  598.9 0.5 add.79
  599.5 0.0 copy-start.5
  599.5 0.0 copy-start.10
  599.5 1.5 collective-permute-start.2
  601.0 0.0 copy-done.7
  601.0 0.0 copy-done.12
  601.0 2.3 convolution_convert_fusion.2
  603.3 4.4 convolution_convert_fusion.3
  607.8 83.5 %collective-permute-done.2 = f32[256,4096]{0,1:T(8,128)S(1)} collective-permute-done((f32[256,4096]{0,1:T(8,128)S(1)}, f32[256,4096]{0,1:T(8,128)S(1)}, u32[]{:S(2)}, u32[]{:S(2)}) %collective-permute-start.2) | collective-permute-done | bytes 4194336 | tf_op jit(solution)/shard_map/ppermute | solution.py:127
  691.3 0.5 add.80
  691.9 1.9 slice_multiply_fusion
  693.7 0.1 slice_multiply_fusion.1
  693.8 3.6 copy.21
  697.4 1.3 copy.22
  698.7 0.0 copy-done.1
  (13 shorter events, 0.0 us)
Async XLA Ops:
  7.2 166.5 %copy-start = (bf16[512,1024]{1,0:T(8,128)(2,1)S(1)}, bf16[512,1024]{1,0:T(8,128)(2,1)}, u32[]{:S(2)}) copy-start(bf16[512,1024]{1,0:T(8,128)(2,1)} %param.7) | copy-start | bytes 3145732
  7.2 50.8 %all-gather.5.cloned.1.call-start = ((), (), s32[]{:S(2)}) async-start(), calls=%async_computation.2 | async-start | bytes 2621440 | tf_op jit(solution)/shard_map/all_gather | solution.py:95
  7.9 165.8 %all-gather.3.cloned.1.call-start = ((), (), s32[]{:S(2)}) async-start(), calls=%async_computation.1 | async-start | bytes 7864320 | tf_op jit(solution)/shard_map/all_gather | solution.py:84
  8.7 487.3 %reduce-scatter.2.cloned.1.call-start = ((), (), s32[]{:S(2)}) async-start(), calls=%async_computation.3 | async-start | bytes 20971520 | tf_op jit(solution)/shard_map/reduce_scatter | solution.py:122
  189.4 6.5 copy-start.2
  189.4 6.7 copy-start.3
  194.2 10.0 %copy-start.11 = (bf16[8,128,512]{2,1,0:T(8,128)(2,1)}, bf16[8,128,512]{2,1,0:T(8,128)(2,1)S(1)}, u32[]{:S(2)}) copy-start(bf16[8,128,512]{2,1,0:T(8,128)(2,1)S(1)} %fusion.9) | copy-start | bytes 3145732
  196.1 1.5 copy-start.6
  197.7 8.6 %copy-start.9 = (bf16[8,128,512]{2,1,0:T(8,128)(2,1)}, bf16[8,128,512]{2,1,0:T(8,128)(2,1)S(1)}, u32[]{:S(2)}) copy-start(bf16[8,128,512]{2,1,0:T(8,128)(2,1)S(1)} %fusion.12) | copy-start | bytes 3145732
  203.4 2.9 copy-start.4
  203.4 1.6 copy-start.8
  495.9 7.4 %collective-permute-start = (f32[256,4096]{0,1:T(8,128)}, f32[256,4096]{0,1:T(8,128)S(1)}, u32[]{:S(2)}, u32[]{:S(2)}) collective-permute-start(f32[256,4096]{0,1:T(8,128)} %reduce-scatter.2.cloned.1.call-done), channel_id=1, source_target_pairs={{0,4},{4,0},{8,12},{12,8},{16,20},{20,16},{24,28},{28,24},{1,5},{5... | collective-permute-start | bytes 12582920 | tf_op jit(solution)/shard_map/ppermute | solution.py:127
  503.3 100.0 %slice-start = ((s8[6291456]{0:T(1024)(128)(4,1)}), s8[4194304]{0:T(1024)(128)(4,1)S(1)}, s32[]{:S(2)}) async-start(s8[6291456]{0:T(1024)(128)(4,1)} %bitcast.76), calls=%async_computation.4 | async-start | bytes 8388608
  506.2 94.8 %copy-start.7 = (bf16[1024,1024]{1,0:T(8,128)(2,1)S(1)}, bf16[1024,1024]{1,0:T(8,128)(2,1)}, u32[]{:S(2)}) copy-start(bf16[1024,1024]{1,0:T(8,128)(2,1)} %all-gather.5.cloned.1.call-done) | copy-start | bytes 6291460
  506.2 94.8 %copy-start.12 = (bf16[8,128,512]{2,1,0:T(8,128)(2,1)S(1)}, bf16[8,128,512]{2,1,0:T(8,128)(2,1)}, u32[]{:S(2)}) copy-start(bf16[8,128,512]{2,1,0:T(8,128)(2,1)} %copy-done.11) | copy-start | bytes 3145732
  506.2 97.1 %slice-start.1 = ((s8[6291456]{0:T(1024)(128)(4,1)}), s8[2097152]{0:T(1024)(128)(4,1)S(1)}, s32[]{:S(2)}) async-start(s8[6291456]{0:T(1024)(128)(4,1)} %bitcast.76), calls=%async_computation.5 | async-start | bytes 4194304
  506.2 92.7 %collective-permute-start.1 = (f32[256,4096]{0,1:T(8,128)S(1)}, f32[256,4096]{0,1:T(8,128)S(1)}, u32[]{:S(2)}, u32[]{:S(2)}) collective-permute-start(f32[256,4096]{0,1:T(8,128)S(1)} %add.78), channel_id=1, source_target_pairs={{0,8},{4,12},{8,0},{12,4},{16,24},{20,28},{24,16},{28,20},{1,9},{5... | collective-permute-start | bytes 12582920 | tf_op jit(solution)/shard_map/ppermute | solution.py:127
  599.5 3.9 copy-start.5
  599.5 3.8 copy-start.10
  599.5 91.8 %collective-permute-start.2 = (f32[256,4096]{0,1:T(8,128)S(1)}, f32[256,4096]{0,1:T(8,128)S(1)}, u32[]{:S(2)}, u32[]{:S(2)}) collective-permute-start(f32[256,4096]{0,1:T(8,128)S(1)} %add.79), channel_id=1, source_target_pairs={{0,16},{4,20},{8,24},{12,28},{16,0},{20,4},{24,8},{28,12},{1,17},{... | collective-permute-start | bytes 12582920 | tf_op jit(solution)/shard_map/ppermute | solution.py:127
  693.7 5.0 copy-start.1
Sparse Core Ops, SparseCore 0:
  9.6 48.3 all-gather.4
  59.5 114.1 all-gather.2
  217.2 278.6 reduce-scatter.1
